TPU v7x, 512 devices: a whole 4x8x8 slice. The times are simulated.
512 devices in a mesh: view: 64 (over y, z), chord: 8 (over x, core).
Axes of the slice: x: 4, y: 8, z: 8, core: 2. Of those that a mesh axis runs over, the one named last changes fastest.
Arguments:
- proj: bfloat16 [768, 4096, 128], P('view', 'chord'), may hold values from -16 to 16
- tiles: bfloat16 [384, 256, 1024], P('view'), may hold values from -0.01953125 to 0.01953125
- owner: int32 [8, 512], replicated, may hold values from 0 to 511, as said below
- lengths: int32 [8, 512], replicated, may hold values from 1 to 1024, as said below
Outputs:
- recon: float32 [8, 512, 1024], P('chord', 'view')
Inputs may be any that keep to these rules, and one draw needn't show every extreme that they name: `owner`: each row is an ordering of the 512 chords of one group. In each group, the lengths of the chords at owner positions k * 8 to k * 8 + 7 sum to at most 4608, exactly 4608 for some k; the largest entry of each row is 1024.
All inputs are finite; a program needn't handle non-finite values.
Results may differ from a plain program's by a relative error of at most 0.0003.
Values sent between devices are 32-bit elements; how exact they have to be, the bound alone decides.
A program may use at most 64 MiB of HBM per device.

v0:
```python
from functools import partial
import math

import jax
import jax.numpy as jnp
from jax import lax
from jax.sharding import PartitionSpec as P

NB = 4


def kernel_table(rows, start, cols):
    row_pos = start + jnp.arange(rows, dtype=jnp.float32)[:, None]
    col_pos = jnp.arange(cols, dtype=jnp.float32)[None, :]
    return 1.0 / (row_pos - col_pos + 0.5)


def weigh(length, count, start):
    position = start + jnp.arange(count, dtype=jnp.float32)[None, :] + 0.5
    inside = position < length
    return (inside, jnp.sqrt(jnp.where(inside, position * (length - position), 1.0)))


def invert_block(sums, length, table, start):
    length = length.astype(jnp.float32)[:, None]
    col_in, col_w = weigh(length, sums.shape[1], 0.0)
    row_in, row_w = weigh(length, table.shape[0], start)
    scaled = jnp.where(col_in, col_w * sums, 0.0)
    image = jnp.dot(
        scaled, table.T, precision=lax.Precision.HIGHEST, preferred_element_type=jnp.float32
    )
    return jnp.where(row_in, image / (math.pi * row_w), 0.0)


def bucket_invert(capacity, table, chord_row, chord_length):
    result = invert_block(
        chord_row[None, :capacity], chord_length[None], table[:capacity, :capacity], 0.0
    )[0]
    return jnp.pad(result, (0, chord_row.shape[0] - capacity))


def per_device(proj, tiles, owner, lengths):
    view_count, group_rows, footprint = proj.shape
    block_count = tiles.shape[0]
    samples = tiles.shape[2]
    block_views = view_count // block_count
    group = lax.axis_index("chord")
    view_place = lax.axis_index("view")
    view_devices = lax.axis_size("view")
    owned = group_rows // view_devices
    my_order = lax.dynamic_index_in_dim(owner, group, 0, keepdims=False)
    data_blocks = proj.reshape(block_count, block_views, group_rows, footprint)
    tile_stack = tiles.reshape(block_count, block_views, footprint, samples)
    ordered_len = jnp.take_along_axis(lengths, owner, axis=1)
    owned_len = lax.dynamic_slice_in_dim(ordered_len, view_place * owned, owned, axis=1)
    my_len = lax.dynamic_index_in_dim(owned_len, group, 0, keepdims=False)
    picked = jnp.take(data_blocks, my_order, axis=2)

    def step(total, inputs):
        views_now, tile = inputs
        return (
            total + jnp.einsum("vkd,vds->ks", views_now, tile, preferred_element_type=jnp.float32),
            None,
        )

    start_total = jnp.zeros((my_order.shape[0], samples), jnp.float32)
    total, _ = lax.scan(step, start_total, (picked, tile_stack))
    chord_totals = lax.psum_scatter(total, "view", scatter_dimension=0, tiled=True)
    table = kernel_table(samples, 0.0, samples)
    branches = [partial(bucket_invert, samples * (level + 1) // NB, table) for level in range(NB)]

    def one_chord(inputs):
        chord_row, chord_length = inputs
        level = jnp.minimum((chord_length - 1) * NB // samples, NB - 1)
        return lax.switch(level, branches, chord_row, chord_length)

    recon = lax.map(one_chord, (chord_totals, my_len))
    return recon[None]


def solution(mesh):
    placed = (P("view", "chord", None), P("view", None, None), P(), P())
    return jax.shard_map(
        per_device, mesh=mesh, in_specs=placed, out_specs=P("chord", "view", None), check_vma=False
    )
```

profile of v0, /device:TPU:12, one launch (start us, length us, event | category | flops | bytes accessed | tf_op | source)
XLA Modules:
  0.0 290.3 jit_solution(14342944208237712963)
XLA Ops:
  6.5 0.7 compare_select_fusion.1
  7.3 4.2 %copy.8 = bf16[6,2,512,128]{3,1,2,0:T(2,128)(2,1)} copy(bf16[6,2,512,128]{3,2,1,0:T(8,128)(2,1)} %bitcast.57) | data formatting | bytes 3145728 | tf_op jit(solution)/shard_map/reshape | solution.py:52
  11.5 7.7 %gather_fusion = bf16[512,6,2,128]{3,2,1,0:T(2,128)(2,1)} fusion(bf16[6,2,512,128]{3,1,2,0:T(2,128)(2,1)} %copy.8, s32[1024]{0:T(1024)S(1)} %pad_clamp_fusion), kind=kCustom, calls=%fused_computation | custom fusion | bytes 3147776 | tf_op jit(solution)/shard_map/jit(_take)/gather | solution.py:57
  19.2 4.6 %fusion.28 = bf16[6,2,512,128]{3,1,0,2:T(2,128)(2,1)} fusion(bf16[512,6,2,128]{3,2,1,0:T(2,128)(2,1)} %gather_fusion, pred[512]{0:T(512)(128)(4,1)S(1)} %compare_and_fusion), kind=kLoop, calls=%fused_computation.52 | loop fusion | flops 786432 | bytes 3146240 | tf_op jit(solution)/shard_map/jit(_take)/select_n | solution.py:57
  23.8 18.0 %while.27 = (s32[]{:T(128)}, f32[512,1024]{1,0:T(8,128)S(1)}, bf16[6,2,512,128]{3,1,0,2:T(2,128)(2,1)}, bf16[6,2,128,1024]{3,2,1,0:T(8,128)(2,1)}, s32[]{:T(128)}, /*index=5*/s32[]{:T(128)}) while((s32[]{:T(128)}, f32[512,1024]{1,0:T(8,128)S(1)}, bf16[6,2,512,128]{3,1,0,2:T(2,128)(2,1)}, bf16[6,2,128,1024]{3,2,1,0:T(8,128)(2,1)}, ...), condition=%wide.region_1.2_spmd.clone, body=%wide.region_0.1_spmd.clone.sunk | while | flops 269484032 | bytes 5505619 | solution.py:67
  23.8 1.1 constant_dynamic-slice_fusion.8
  24.9 1.8 bitcast_add_fusion.2
  26.8 1.1 constant_dynamic-slice_fusion.8
  27.9 1.8 bitcast_add_fusion.2
  29.8 1.1 constant_dynamic-slice_fusion.8
  30.9 1.8 bitcast_add_fusion.2
  32.8 1.1 constant_dynamic-slice_fusion.8
  33.9 1.8 bitcast_add_fusion.2
  35.8 1.1 constant_dynamic-slice_fusion.8
  36.9 1.8 bitcast_add_fusion.2
  38.8 1.1 constant_dynamic-slice_fusion.8
  39.9 1.8 bitcast_add_fusion.2
  41.8 1.3 copy-done.1
  43.2 25.5 %gather_fusion.1 = s32[4096]{0:T(1024)S(1)} fusion(s32[8,512]{1,0:T(8,128)S(1)} %copy-done, s32[4096]{0:T(1024)S(1)} %bitcast.55), kind=kCustom, calls=%fused_computation.1 | custom fusion | bytes 65536 | tf_op jit(solution)/shard_map/jit(take_along_axis)/gather | solution.py:54
  68.7 1.3 dynamic-slice
  70.5 0.1 fusion.30
  70.6 140.3 %all-reduce.6.cloned.1.call-done = f32[512,1024]{1,0:T(8,128)} async-done(((f32[512,1024]{1,0:T(8,128)}), f32[512,1024]{1,0:T(8,128)}) %all-reduce.6.cloned.1.call-update) | async-done | bytes 2097168
  210.9 0.8 constant_dynamic-slice_fusion.4
  211.7 71.8 %while.26 = (s32[]{:T(128)}, f32[8,1024]{1,0:T(8,128)}, s32[8]{0:T(128)S(1)}, f32[8,1024]{1,0:T(8,128)S(1)}, s32[]{:T(128)}, /*index=5*/s32[]{:T(128)}, s32[]{:T...) while((s32[]{:T(128)}, f32[8,1024]{1,0:T(8,128)}, s32[8]{0:T(128)S(1)}, ...), condition=%wide.region_8.9_spmd.clone.clone, body=%wide.region_3.8_spmd.clone.clone.sunk | while | flops 15744022 | bytes 8429955 | solution.py:77
  211.7 0.6 dynamic_slice.73
  212.9 2.6 add_divide_fusion.2
  215.5 1.9 conditional.4
  216.1 1.2 fusion.2
  217.4 1.4 dynamic_update_slice.11
  218.8 0.6 dynamic_slice.73
  220.0 2.6 add_divide_fusion.2
  222.6 4.3 %conditional.4 = (f32[1,1024]{1,0:T(1,128)S(1)}) conditional(s32[]{:T(128)} %clamp.21, (s32[]{:T(128)}, f32[8,1024]{1,0:T(8,128)S(1)}, s32[]{:T(128)}, f32[1024,1024]{1,0:T(8,128)}) %tuple.86, (s32[]{:T(128)}, f32[8,1024]{1,0:T(8,128)S(1)}, s32[]{:T(128)}, f32[1024,1024]{1,0:T(8,128)}) %tuple.86, (s32[]{:T(128)}, ...), branch_computations={%region_4.4_spmd, %region_5.5_spmd, %region_6.6_spmd, %region_7.7_... | conditional | flops 12598273 | bytes 4227100 | solution.py:75
  223.2 3.7 %fusion.22 = f32[768]{0:T(1024)S(1)} fusion(f32[768,1]{0,1:T(1,128)S(1)} %reshape.169, f32[1024,1024]{1,0:T(8,128)} %get-tuple-element.206), kind=kOutput, calls=%fused_computation.41 | convolution fusion | flops 7077888 | bytes 2365440 | tf_op jit(solution)/shard_map/while/body/eval_jaxpr/cond/branch_2_fun/dot_general | solution.py:29
  226.9 1.4 dynamic_update_slice.11
  228.3 0.6 dynamic_slice.73
  229.5 2.6 add_divide_fusion.2
  232.1 4.3 %conditional.4 = (f32[1,1024]{1,0:T(1,128)S(1)}) conditional(s32[]{:T(128)} %clamp.21, (s32[]{:T(128)}, f32[8,1024]{1,0:T(8,128)S(1)}, s32[]{:T(128)}, f32[1024,1024]{1,0:T(8,128)}) %tuple.86, (s32[]{:T(128)}, f32[8,1024]{1,0:T(8,128)S(1)}, s32[]{:T(128)}, f32[1024,1024]{1,0:T(8,128)}) %tuple.86, (s32[]{:T(128)}, ...), branch_computations={%region_4.4_spmd, %region_5.5_spmd, %region_6.6_spmd, %region_7.7_... | conditional | flops 12598273 | bytes 4227100 | solution.py:75
  232.7 3.7 %fusion.22 = f32[768]{0:T(1024)S(1)} fusion(f32[768,1]{0,1:T(1,128)S(1)} %reshape.169, f32[1024,1024]{1,0:T(8,128)} %get-tuple-element.206), kind=kOutput, calls=%fused_computation.41 | convolution fusion | flops 7077888 | bytes 2365440 | tf_op jit(solution)/shard_map/while/body/eval_jaxpr/cond/branch_2_fun/dot_general | solution.py:29
  236.4 1.4 dynamic_update_slice.11
  237.8 0.6 dynamic_slice.73
  239.0 2.6 add_divide_fusion.2
  241.6 4.3 %conditional.4 = (f32[1,1024]{1,0:T(1,128)S(1)}) conditional(s32[]{:T(128)} %clamp.21, (s32[]{:T(128)}, f32[8,1024]{1,0:T(8,128)S(1)}, s32[]{:T(128)}, f32[1024,1024]{1,0:T(8,128)}) %tuple.86, (s32[]{:T(128)}, f32[8,1024]{1,0:T(8,128)S(1)}, s32[]{:T(128)}, f32[1024,1024]{1,0:T(8,128)}) %tuple.86, (s32[]{:T(128)}, ...), branch_computations={%region_4.4_spmd, %region_5.5_spmd, %region_6.6_spmd, %region_7.7_... | conditional | flops 12598273 | bytes 4227100 | solution.py:75
  242.2 3.7 %fusion.22 = f32[768]{0:T(1024)S(1)} fusion(f32[768,1]{0,1:T(1,128)S(1)} %reshape.169, f32[1024,1024]{1,0:T(8,128)} %get-tuple-element.206), kind=kOutput, calls=%fused_computation.41 | convolution fusion | flops 7077888 | bytes 2365440 | tf_op jit(solution)/shard_map/while/body/eval_jaxpr/cond/branch_2_fun/dot_general | solution.py:29
  246.0 1.4 dynamic_update_slice.11
  247.4 0.6 dynamic_slice.73
  248.5 2.6 add_divide_fusion.2
  251.1 2.8 conditional.4
  251.7 2.2 fusion.8
  254.0 1.4 dynamic_update_slice.11
  255.4 0.6 dynamic_slice.73
  256.5 2.6 add_divide_fusion.2
  259.1 4.3 %conditional.4 = (f32[1,1024]{1,0:T(1,128)S(1)}) conditional(s32[]{:T(128)} %clamp.21, (s32[]{:T(128)}, f32[8,1024]{1,0:T(8,128)S(1)}, s32[]{:T(128)}, f32[1024,1024]{1,0:T(8,128)}) %tuple.86, (s32[]{:T(128)}, f32[8,1024]{1,0:T(8,128)S(1)}, s32[]{:T(128)}, f32[1024,1024]{1,0:T(8,128)}) %tuple.86, (s32[]{:T(128)}, ...), branch_computations={%region_4.4_spmd, %region_5.5_spmd, %region_6.6_spmd, %region_7.7_... | conditional | flops 12598273 | bytes 4227100 | solution.py:75
  259.8 3.7 %fusion.22 = f32[768]{0:T(1024)S(1)} fusion(f32[768,1]{0,1:T(1,128)S(1)} %reshape.169, f32[1024,1024]{1,0:T(8,128)} %get-tuple-element.206), kind=kOutput, calls=%fused_computation.41 | convolution fusion | flops 7077888 | bytes 2365440 | tf_op jit(solution)/shard_map/while/body/eval_jaxpr/cond/branch_2_fun/dot_general | solution.py:29
  263.5 1.4 dynamic_update_slice.11
  264.9 0.6 dynamic_slice.73
  266.0 2.6 add_divide_fusion.2
  268.7 1.9 conditional.4
  269.3 1.2 fusion.2
  270.6 1.4 dynamic_update_slice.11
  272.0 0.6 dynamic_slice.73
  273.1 2.6 add_divide_fusion.2
  275.8 6.3 %conditional.4 = (f32[1,1024]{1,0:T(1,128)S(1)}) conditional(s32[]{:T(128)} %clamp.21, (s32[]{:T(128)}, f32[8,1024]{1,0:T(8,128)S(1)}, s32[]{:T(128)}, f32[1024,1024]{1,0:T(8,128)}) %tuple.86, (s32[]{:T(128)}, f32[8,1024]{1,0:T(8,128)S(1)}, s32[]{:T(128)}, f32[1024,1024]{1,0:T(8,128)}) %tuple.86, (s32[]{:T(128)}, ...), branch_computations={%region_4.4_spmd, %region_5.5_spmd, %region_6.6_spmd, %region_7.7_... | conditional | flops 12598273 | bytes 4227100 | solution.py:75
  276.4 5.6 %fusion.31 = f32[1,1024]{1,0:T(1,128)S(1)} fusion(f32[1024,1]{0,1:T(1,128)S(1)} %bitcast.64, f32[1024,1024]{1,0:T(8,128)} %get-tuple-element.210), kind=kOutput, calls=%fused_computation.64 | convolution fusion | flops 12582912 | bytes 4202496 | tf_op jit(solution)/shard_map/while/body/eval_jaxpr/cond/branch_3_fun/dot_general | solution.py:29
  282.0 1.4 dynamic_update_slice.11
  (50 shorter events, 0.7 us)
Async XLA Ops:
  6.5 36.6 %copy-start = (s32[8,512]{1,0:T(8,128)S(1)}, s32[8,512]{1,0:T(8,128)}, u32[]{:S(2)}) copy-start(s32[8,512]{1,0:T(8,128)} %param.15) | copy-start | bytes 49156
  6.5 204.4 %all-reduce.6.cloned.1.call-start = ((), (), s32[]{:S(2)}) async-start(), calls=%async_computation | async-start | bytes 4194304
  41.8 1.3 copy-start.1
  41.8 1.4 copy-start.2
Sparse Core Ops, SparseCore 0:
  43.2 167.6 all-reduce.5
where the time goes:
time: 292 us; the launch traced here: 290 us
  waiting for transfers between devices  140 us (48%)
  local copies, waits for them, and re-layouts  63.5 us (22%)
  matrix products  35.9 us (12%)
  other arithmetic  26.8 us (9%)
  between operations  14.1 us (5%)
  loops' own time  9.73 us (3%)
    unnamed x2, waiting for transfers between devices  140 us
    gather x2, local copies, waits for them, and re-layouts, per_device(): ordered_len = jnp.take_along_axis(lengths, owner, axis=1)  25.5 us
    dot_general x8, matrix products, invert_block(): jnp.dot(scaled, table.T, precision=lax.Precision.HIGHEST, preferred_eleme...  24.9 us
    div x8, other arithmetic, kernel_table(): return 1.0 / (row_pos - col_pos + 0.5)  20.9 us
    dynamic_update_slice x8, local copies, waits for them, and re-layouts, per_device(): recon = lax.map(one_chord, (chord_totals, my_len))  11.2 us
    dot_general x6, matrix products, step(): jnp.einsum('vkd,vds->ks', views_now, tile, preferred_element_type=jnp.flo...  11 us
    gather x1, local copies, waits for them, and re-layouts, per_device(): picked = jnp.take(data_blocks, my_order, axis=2)  7.69 us
    dynamic_slice x6, local copies, waits for them, and re-layouts, per_device(): total, _ = lax.scan(step, start_total, (picked, tile_stack))  6.81 us
  transfers between devices with their start and end apart: 1, of which 1 were waited for; matrix products, arithmetic and copies ran while one was open for 9% of the time, Pallas kernels for 0%

commit v1 on v0

v1 whole, which is shorter than its diff:
```python
import math

import jax
import jax.numpy as jnp
from jax import lax
from jax.sharding import PartitionSpec as P

LANES = 128
PACK = 4608


def kernel_table(rows, start, cols):
    row_pos = start + jnp.arange(rows, dtype=jnp.float32)[:, None]
    col_pos = jnp.arange(cols, dtype=jnp.float32)[None, :]
    return 1.0 / (row_pos - col_pos + 0.5)


def weigh(length, count, start):
    position = start + jnp.arange(count, dtype=jnp.float32)[None, :] + 0.5
    inside = position < length
    return (inside, jnp.sqrt(jnp.where(inside, position * (length - position), 1.0)))


def invert_block(sums, length, table, start):
    length = length.astype(jnp.float32)[:, None]
    col_in, col_w = weigh(length, sums.shape[1], 0.0)
    row_in, row_w = weigh(length, table.shape[0], start)
    scaled = jnp.where(col_in, col_w * sums, 0.0)
    image = jnp.dot(
        scaled, table.T, precision=lax.Precision.HIGHEST, preferred_element_type=jnp.float32
    )
    return jnp.where(row_in, image / (math.pi * row_w), 0.0)


def chunk_plan(order_len, per_owner, chunks_per_row, slots):
    counts = (order_len + LANES - 1) // LANES
    ends = jnp.cumsum(counts, axis=1)
    starts = ends - counts
    slot = jnp.arange(slots, dtype=jnp.int32)
    member = jnp.sum(ends[:, None, :] <= slot[None, :, None], axis=2)
    member = jnp.minimum(member, per_owner - 1)
    first = jnp.take_along_axis(starts, member, axis=1)
    within = jnp.clip(slot[None, :] - first, 0, chunks_per_row - 1)
    return starts, member, within


def per_device(proj, tiles, owner, lengths):
    view_count, group_rows, footprint = proj.shape
    samples = tiles.shape[2]
    group = lax.axis_index("chord")
    view_place = lax.axis_index("view")
    view_devices = lax.axis_size("view")
    owned = group_rows // view_devices
    chunks_per_row = samples // LANES
    slots = min(chunks_per_row * owned, (PACK + owned * (LANES - 1)) // LANES)

    tile_rows = tiles.reshape(view_count, footprint, samples)
    sums = jnp.einsum("vkd,vds->ks", proj, tile_rows, preferred_element_type=jnp.float32)

    my_order = lax.dynamic_index_in_dim(owner, group, 0, keepdims=False)
    my_lengths = lax.dynamic_index_in_dim(lengths, group, 0, keepdims=False)
    order_len = jnp.take(my_lengths, my_order).reshape(view_devices, owned)
    order_rows = my_order.reshape(view_devices, owned)
    starts, member, within = chunk_plan(order_len, owned, chunks_per_row, slots)
    src_row = jnp.take_along_axis(order_rows, member, axis=1)
    src = src_row * chunks_per_row + within
    flat = sums.reshape(group_rows * chunks_per_row, LANES)
    packed = jnp.take(flat, src.reshape(-1), axis=0).reshape(view_devices, slots, LANES)

    mine = lax.psum_scatter(packed, "view", scatter_dimension=0, tiled=True)[0]

    my_starts = lax.dynamic_index_in_dim(starts, view_place, 0, keepdims=False)
    my_len = lax.dynamic_index_in_dim(order_len, view_place, 0, keepdims=False)
    back = my_starts[:, None] + jnp.arange(chunks_per_row, dtype=jnp.int32)[None, :]
    back = jnp.minimum(back, slots - 1)
    rows = jnp.take(mine, back.reshape(-1), axis=0).reshape(owned, samples)

    table = kernel_table(samples, 0.0, samples)
    recon = invert_block(rows, my_len, table, 0.0)
    return recon[None]


def solution(mesh):
    placed = (P("view", "chord", None), P("view", None, None), P(), P())
    return jax.shard_map(
        per_device, mesh=mesh, in_specs=placed, out_specs=P("chord", "view", None), check_vma=False
    )
```

time: 292 us -> 332 us (1.14)
  the two profiles are of different devices: /device:TPU:12 before, /device:TPU:6 now
where the time goes in v1:
time: 332 us
  waiting for transfers between devices  249 us (75%)
  local copies, waits for them, and re-layouts  55.8 us (17%)
  between operations  13.5 us (4%)
  matrix products  8.84 us (3%)
  other arithmetic  3.9 us (1%)
    unnamed x2, waiting for transfers between devices  249 us
    gather x5, local copies, waits for them, and re-layouts, per_device(): src_row = jnp.take_along_axis(order_rows, member, axis=1)  17.5 us
    gather x3, local copies, waits for them, and re-layouts, chunk_plan(): first = jnp.take_along_axis(starts, member, axis=1)  17.3 us
    gather x2, local copies, waits for them, and re-layouts, per_device(): jnp.take(flat, src.reshape(-1), axis=0).reshape(view_devices, slots, LANES)  10 us
  transfers between devices with their start and end apart: 1, of which 1 were waited for; matrix products, arithmetic and copies ran while one was open for 0% of the time, Pallas kernels for 0%

profile of v1, /device:TPU:6, one launch (start us, length us, event | category | flops | bytes accessed | tf_op | source)
XLA Modules:
  0.0 331.6 jit_solution(5984636396191572275)
XLA Ops:
  6.5 0.0 copy-start
  6.5 0.0 reduce-scatter.4.cloned.1.call-start
  6.5 1.9 copy-done
  8.4 4.5 %convolution_bitcast_fusion = f32[512,1024]{1,0:T(8,128)} fusion(bf16[12,512,128]{2,1,0:T(8,128)(2,1)} %param.6, bf16[12,128,1024]{2,1,0:T(8,128)(2,1)S(1)} %bitcast.29), kind=kOutput, calls=%fused_computation.9 | convolution fusion | flops 1610612736 | bytes 6815744 | tf_op jit(solution)/shard_map/vkd,vds->ks/dot_general | solution.py:58
  12.9 2.7 reshape.158
  15.7 0.7 compare_select_fusion.7
  16.4 0.8 constant_dynamic-slice_fusion.2
  17.1 3.5 %gather_fusion = s32[512]{0:T(512)S(1)} fusion(s32[512]{0:T(512)S(1)} %bitcast.30, s32[1024]{0:T(1024)S(1)} %pad_clamp_fusion.2), kind=kCustom, calls=%fused_computation.2 | custom fusion | bytes 6144 | tf_op jit(solution)/shard_map/jit(_take)/gather | solution.py:62
  20.6 0.1 gather.22
  20.7 0.1 squeeze.15
  20.9 0.2 reduce_window_sum.11
  21.0 0.1 copy.9
  21.1 0.1 convert_reduce_fusion
  21.2 0.1 copy.10
  21.3 0.1 reshape.208
  21.5 17.1 %gather_fusion.3 = s32[2752]{0:T(1024)S(1)} fusion(s32[64,8]{1,0:T(8,128)S(1)} %squeeze.15, s32[2752]{0:T(1024)S(1)} %reshape.208), kind=kCustom, calls=%fused_computation.clone | custom fusion | bytes 44032 | tf_op jit(solution)/shard_map/jit(take_along_axis)/gather | solution.py:65
  38.6 17.1 %gather_fusion.4 = s32[2752]{0:T(1024)S(1)} fusion(s32[64,8]{1,0:T(8,128)S(1)} %fusion.33, s32[2752]{0:T(1024)S(1)} %reshape.208), kind=kCustom, calls=%fused_computation.1.clone | custom fusion | bytes 44032 | tf_op jit(solution)/shard_map/jit(take_along_axis)/gather | solution.py:42
  55.7 0.1 reshape.216
  55.8 0.1 copy.13
  55.9 0.1 reshape.211
  56.0 0.1 copy.11
  56.2 0.1 copy.15
  56.2 0.1 reshape.159
  56.5 7.5 %gather_fusion.1 = f32[2752,128]{1,0:T(8,128)} fusion(f32[4096,128]{1,0:T(8,128)} %reshape.158, s32[3072]{0:T(1024)S(1)} %pad_clamp_fusion), kind=kCustom, calls=%fused_computation.3 | custom fusion | bytes 2829056 | tf_op jit(solution)/shard_map/jit(_take)/gather | solution.py:68
  64.0 2.5 gather.24
  66.5 0.1 copy.14
  66.6 2.6 broadcast_select_fusion
  69.2 0.0 reduce-scatter.4.cloned.1.call-update
  69.2 0.1 add_minimum_fusion
  69.3 0.1 min.37
  69.4 0.1 compare_and_fusion.1
  69.4 0.1 copy.8
  69.6 249.5 %reduce-scatter.4.cloned.1.call-done = f32[1,43,128]{2,1,0:T(8,128)} async-done(((f32[64,43,128]{2,1,0:T(8,128)}), f32[1,43,128]{2,1,0:T(8,128)}) %reduce-scatter.4.cloned.1.call-update) | async-done | bytes 22032
  319.0 1.3 gather_fusion.2
  320.4 4.4 %fusion.5 = f32[1,8,1024]{2,1,0:T(8,128)} fusion(f32[8,1024]{1,0:T(8,128)S(1)} %gather.26, f32[1024]{0:T(1024)S(1)} %iota_add_fusion, f32[8]{0:T(128)S(1)} %fusion.26, pred[8,8]{0,1:T(8,128)(4,1)S(1)} %copy.8), kind=kOutput, calls=%fused_computation.12 | convolution fusion | flops 103923712 | bytes 69728 | tf_op jit(solution)/shard_map/dot_general | solution.py:29
  (13 shorter events, 0.2 us)
Async XLA Ops:
  6.5 1.9 copy-start
  6.5 312.5 %reduce-scatter.4.cloned.1.call-start = ((), (), s32[]{:S(2)}) async-start(), calls=%async_computation.1 | async-start | bytes 1597440
Sparse Core Ops, SparseCore 0:
  69.3 249.6 reduce-scatter.3

commit v2 on v1

v2 whole, which is shorter than its diff:
```python
import functools
import math

import jax
import jax.numpy as jnp
from jax import lax
from jax.experimental import pallas as pl
from jax.experimental.pallas import tpu as pltpu
from jax.sharding import PartitionSpec as P

LANES = 128
PACK = 4608
MESH = pl.DeviceIdType.MESH


def kernel_table(rows, start, cols):
    row_pos = start + jnp.arange(rows, dtype=jnp.float32)[:, None]
    col_pos = jnp.arange(cols, dtype=jnp.float32)[None, :]
    return 1.0 / (row_pos - col_pos + 0.5)


def weigh(length, count, start):
    position = start + jnp.arange(count, dtype=jnp.float32)[None, :] + 0.5
    inside = position < length
    return (inside, jnp.sqrt(jnp.where(inside, position * (length - position), 1.0)))


def invert_block(sums, length, table, start):
    length = length.astype(jnp.float32)[:, None]
    col_in, col_w = weigh(length, sums.shape[1], 0.0)
    row_in, row_w = weigh(length, table.shape[0], start)
    scaled = jnp.where(col_in, col_w * sums, 0.0)
    image = jnp.dot(
        scaled, table.T, precision=lax.Precision.HIGHEST, preferred_element_type=jnp.float32
    )
    return jnp.where(row_in, image / (math.pi * row_w), 0.0)


def pick(table, index):
    hit = index[:, :, None] == jnp.arange(table.shape[1], dtype=jnp.int32)
    return jnp.sum(jnp.where(hit, table[:, None, :], 0), axis=-1)


def ring_phase(n, me, send_right, send_left, chunk, own, recv_r, recv_l, send_r, send_l, ssem, rsem, base):
    nr = n // 2
    nl = n - 1 - nr
    for s in range(max(nr, nl)):
        copies = []
        for go, steps, to, recv, send, sem in (
            (1, nr, send_right, recv_r, send_r, base + s),
            (-1, nl, send_left, recv_l, send_l, base + nr + s),
        ):
            if s >= steps:
                continue
            dest = lax.rem(me + go * (steps - s) + 2 * n, n)
            if s == 0:
                src = chunk(dest)
            else:
                send[s] = recv[s - 1] + own(dest)
                src = send.at[s]
            copy = pltpu.make_async_remote_copy(
                src_ref=src,
                dst_ref=recv.at[s],
                send_sem=ssem.at[sem],
                recv_sem=rsem.at[sem],
                device_id=to,
                device_id_type=MESH,
            )
            copy.start()
            copies.append(copy)
        for copy in copies:
            copy.wait()
    return recv_r.at[nr - 1], recv_l.at[nl - 1]


def rs_kernel(ny, nz, x_ref, o_ref, s1, rr1, rl1, sr1, sl1, rr2, rl2, sr2, sl2, ssem, rsem):
    view = lax.axis_index("view")
    group = lax.axis_index("chord")
    y = view // nz
    z = lax.rem(view, nz)

    def dev(yy, zz):
        return (yy * nz + zz, group)

    z_right = dev(y, lax.rem(z + 1, nz))
    z_left = dev(y, lax.rem(z + nz - 1, nz))
    y_right = dev(lax.rem(y + 1, ny), z)
    y_left = dev(lax.rem(y + ny - 1, ny), z)

    barrier = pltpu.get_barrier_semaphore()
    for peer in (z_right, z_left, y_right, y_left):
        pl.semaphore_signal(barrier, inc=1, device_id=peer, device_id_type=MESH)
    pl.semaphore_wait(barrier, 4)

    fin_r, fin_l = ring_phase(
        nz, z, z_right, z_left,
        lambda d: x_ref.at[d], lambda d: x_ref[d],
        rr1, rl1, sr1, sl1, ssem, rsem, 0,
    )
    s1[...] = x_ref[z] + fin_r[...] + fin_l[...]
    fin_r, fin_l = ring_phase(
        ny, y, y_right, y_left,
        lambda d: s1.at[d], lambda d: s1[d],
        rr2, rl2, sr2, sl2, ssem, rsem, nz - 1,
    )
    o_ref[...] = s1[y] + fin_r[...] + fin_l[...]


def reduce_scatter(packed, ny, nz):
    rows = packed.shape[2]
    nr1, nl1 = nz // 2, nz - 1 - nz // 2
    nr2, nl2 = ny // 2, ny - 1 - ny // 2
    block = (rows, LANES)
    f32 = jnp.float32
    return pl.pallas_call(
        functools.partial(rs_kernel, ny, nz),
        out_shape=jax.ShapeDtypeStruct(block, f32),
        in_specs=[pl.BlockSpec(memory_space=pltpu.VMEM)],
        out_specs=pl.BlockSpec(memory_space=pltpu.VMEM),
        scratch_shapes=[
            pltpu.VMEM((ny,) + block, f32),
            pltpu.VMEM((nr1, ny) + block, f32),
            pltpu.VMEM((nl1, ny) + block, f32),
            pltpu.VMEM((nr1, ny) + block, f32),
            pltpu.VMEM((nl1, ny) + block, f32),
            pltpu.VMEM((nr2,) + block, f32),
            pltpu.VMEM((nl2,) + block, f32),
            pltpu.VMEM((nr2,) + block, f32),
            pltpu.VMEM((nl2,) + block, f32),
            pltpu.SemaphoreType.DMA((nz + ny - 2,)),
            pltpu.SemaphoreType.DMA((nz + ny - 2,)),
        ],
        compiler_params=pltpu.CompilerParams(collective_id=0, has_side_effects=True),
    )(packed)


def per_device(ny, nz, proj, tiles, owner, lengths):
    view_count, group_rows, footprint = proj.shape
    samples = tiles.shape[2]
    group = lax.axis_index("chord")
    view_place = lax.axis_index("view")
    view_devices = ny * nz
    owned = group_rows // view_devices
    chunks_per_row = samples // LANES
    slots = min(chunks_per_row * owned, (PACK + owned * (LANES - 1)) // LANES)

    tile_rows = tiles.reshape(view_count, footprint, samples)
    sums = jnp.einsum("vkd,vds->ks", proj, tile_rows, preferred_element_type=jnp.float32)

    my_order = lax.dynamic_index_in_dim(owner, group, 0, keepdims=False)
    my_lengths = lax.dynamic_index_in_dim(lengths, group, 0, keepdims=False)
    order_len = pick(my_lengths[None, :], my_order[None, :])
    order_len = order_len.reshape(view_devices, owned)
    order_rows = my_order.reshape(view_devices, owned)

    counts = (order_len + LANES - 1) // LANES
    ends = jnp.cumsum(counts, axis=1)
    starts = ends - counts
    slot = jnp.arange(slots, dtype=jnp.int32)
    member = jnp.sum((ends[:, None, :] <= slot[None, :, None]).astype(jnp.int32), axis=2)
    member = jnp.minimum(member, owned - 1)
    first = pick(starts, member)
    src_row = pick(order_rows, member)
    within = jnp.clip(slot[None, :] - first, 0, chunks_per_row - 1)
    src = src_row * chunks_per_row + within
    src = src.reshape(ny, nz, slots).transpose(1, 0, 2)
    flat = sums.reshape(group_rows * chunks_per_row, LANES)
    packed = jnp.take(flat, src.reshape(-1), axis=0).reshape(nz, ny, slots, LANES)

    mine = reduce_scatter(packed, ny, nz)

    my_starts = lax.dynamic_index_in_dim(starts, view_place, 0, keepdims=False)
    my_len = lax.dynamic_index_in_dim(order_len, view_place, 0, keepdims=False)
    back = my_starts[:, None] + jnp.arange(chunks_per_row, dtype=jnp.int32)[None, :]
    back = jnp.minimum(back, slots - 1)
    rows = jnp.take(mine, back.reshape(-1), axis=0).reshape(owned, samples)

    table = kernel_table(samples, 0.0, samples)
    recon = invert_block(rows, my_len, table, 0.0)
    return recon[None]


def solution(mesh):
    view_devices = mesh.shape["view"]
    ny = int(round(math.sqrt(view_devices)))
    nz = view_devices // ny
    placed = (P("view", "chord", None), P("view", None, None), P(), P())
    return jax.shard_map(
        functools.partial(per_device, ny, nz),
        mesh=mesh,
        in_specs=placed,
        out_specs=P("chord", "view", None),
        check_vma=False,
    )
```

time: 332 us -> 80.1 us (0.24)
  waiting for transfers between devices: 249 us -> 0 us
  Pallas kernels: 0 us -> 48.4 us
  local copies, waits for them, and re-layouts: 55.8 us -> 18.7 us
  between operations: 13.5 us -> 0.14 us
    unnamed x2 -> x0, waiting for transfers between devices: 249 us -> none
    pallas_call x0 -> x1, Pallas kernels: none -> 48.4 us  [reduce_scatter(): pl.pallas_call(functools.partial(rs_kernel, ny, nz), out_shape=jax.ShapeD...]
    gather x12 -> x2, local copies, waits for them, and re-layouts: 48.4 us -> 10 us  [per_device(): jnp.take(flat, src.reshape(-1), axis=0).reshape(nz, ny, slots, LANES)]
  transfers between devices with their start and end apart: 1 -> 0, of which waited for: 1 -> 0; matrix products, arithmetic and copies ran while one was open for 0% -> 0% of each run, Pallas kernels for 0% -> 0%
where the time goes in v2:
time: 80.1 us; the launch traced here: 79.7 us
  Pallas kernels  48.4 us (60%)
  local copies, waits for them, and re-layouts  18.7 us (23%)
  matrix products  8.85 us (11%)
  other arithmetic  3.56 us (4%)
    pallas_call x1, Pallas kernels, reduce_scatter(): pl.pallas_call(functools.partial(rs_kernel, ny, nz), out_shape=jax.ShapeD...  48.4 us
    gather x2, local copies, waits for them, and re-layouts, per_device(): jnp.take(flat, src.reshape(-1), axis=0).reshape(nz, ny, slots, LANES)  10 us
    dot_general x1, matrix products, per_device(): jnp.einsum('vkd,vds->ks', proj, tile_rows, preferred_element_type=jnp.flo...  4.49 us
    dot_general x1, matrix products, invert_block(): jnp.dot(scaled, table.T, precision=lax.Precision.HIGHEST, preferred_eleme...  4.35 us
    reshape x1, local copies, waits for them, and re-layouts, per_device(): flat = sums.reshape(group_rows * chunks_per_row, LANES)  2.74 us
    select_n x2, other arithmetic, per_device(): jnp.take(flat, src.reshape(-1), axis=0).reshape(nz, ny, slots, LANES)  2.64 us
    dynamic_slice x2, local copies, waits for them, and re-layouts, per_device(): my_order = lax.dynamic_index_in_dim(owner, group, 0, keepdims=False)  1.91 us
    unnamed x2, local copies, waits for them, and re-layouts  1.89 us

profile of v2, /device:TPU:6, one launch (start us, length us, event | category | flops | bytes accessed | tf_op | source)
XLA Modules:
  0.0 79.7 jit_solution(18169763473882181034)
XLA Ops:
  0.0 0.0 copy-start
  0.0 1.9 %copy-done = bf16[6,256,1024]{2,1,0:T(8,128)(2,1)S(1)} copy-done((bf16[6,256,1024]{2,1,0:T(8,128)(2,1)S(1)}, bf16[6,256,1024]{2,1,0:T(8,128)(2,1)}, u32[]{:S(2)}) %copy-start) | copy-done | bytes 3145752
  1.9 4.5 %convolution_bitcast_fusion = f32[512,1024]{1,0:T(8,128)} fusion(bf16[12,512,128]{2,1,0:T(8,128)(2,1)} %param.4, bf16[12,128,1024]{2,1,0:T(8,128)(2,1)S(1)} %bitcast.29), kind=kOutput, calls=%fused_computation.6 | convolution fusion | flops 1610612736 | bytes 6815744 | tf_op jit(solution)/shard_map/vkd,vds->ks/dot_general | solution.py:148
  6.4 2.7 %reshape.226 = f32[4096,128]{1,0:T(8,128)} reshape(f32[512,1024]{1,0:T(8,128)} %convolution_bitcast_fusion) | data formatting | bytes 4194304 | tf_op jit(solution)/shard_map/reshape | solution.py:167
  9.1 0.5 broadcast.216
  9.6 1.4 %fusion.34 = (s32[512]{0:T(512)S(1)}, s32[1,512]{1,0:T(1,128)S(1)}, s32[1,512]{1,0:T(1,128)S(1)}) fusion(s32[]{:T(128)} %broadcast.216, s32[8,512]{1,0:T(8,128)} %param.6, s32[]{:T(128)S(6)} %select_n.93, s32[8,512]{1,0:T(8,128)} %param.7), kind=kLoop, calls=%fused_computation.69 | loop fusion | bytes 10248 | tf_op jit(solution)/shard_map/jit(dynamic_index_in_dim)/dynamic_slice | solution.py:150
  11.0 0.2 select_reduce_fusion
  11.3 0.1 reshape.224
  11.4 0.2 reduce_window_sum.11
  11.6 0.1 copy.20
  11.7 0.1 copy.17
  11.7 0.1 convert_reduce_fusion
  11.8 0.1 broadcast_in_dim.90
  11.9 0.1 copy.18
  12.0 0.1 select_reduce_fusion.1
  12.1 0.1 copy.21
  12.2 0.1 copy.19
  12.4 0.1 reshape.227
  12.6 7.5 %gather_fusion = f32[2752,128]{1,0:T(8,128)} fusion(f32[4096,128]{1,0:T(8,128)} %reshape.226, s32[3072]{0:T(1024)S(1)} %pad_clamp_fusion), kind=kCustom, calls=%fused_computation | custom fusion | bytes 2829056 | tf_op jit(solution)/shard_map/jit(_take)/gather | solution.py:168
  20.1 2.5 %gather.13 = f32[8,8,43,128]{3,2,1,0:T(8,128)} reshape(f32[2752,128]{1,0:T(8,128)} %gather_fusion) | data formatting | bytes 2818048 | tf_op jit(solution)/shard_map/jit(_take)/gather | solution.py:168
  22.6 2.6 %broadcast_select_fusion.x_ref = f32[8,8,43,128]{3,2,1,0:T(8,128)} fusion(f32[8,8,43,128]{3,2,1,0:T(8,128)} %gather.13, pred[8,8,43]{2,1,0:T(8,128)(4,1)S(1)} %copy.24), kind=kLoop, calls=%fused_computation.12 | loop fusion | flops 352256 | bytes 2820800 | tf_op jit(solution)/shard_map/jit(_take)/select_n | solution.py:168
  25.2 48.4 %shard_map.46 = f32[43,128]{1,0:T(8,128)} custom-call(f32[8,8,43,128]{3,2,1,0:T(8,128)} %broadcast_select_fusion.x_ref), custom_call_target="tpu_custom_call" | custom-call | tf_op jit(solution)/shard_map/pallas_call | solution.py:115
  73.6 0.1 add_minimum_fusion
  73.6 0.1 min.44
  73.7 1.3 %gather_fusion.1 = f32[64,128]{1,0:T(8,128)S(1)} fusion(f32[43,128]{1,0:T(8,128)} %shard_map.46, s32[1024]{0:T(1024)S(1)} %pad_clamp_fusion.1), kind=kCustom, calls=%fused_computation.1 | custom fusion | bytes 65792 | tf_op jit(solution)/shard_map/jit(_take)/gather | solution.py:176
  75.1 0.1 compare_and_fusion.1
  75.2 0.1 copy.16
  75.3 4.4 %fusion.5 = f32[1,8,1024]{2,1,0:T(8,128)} fusion(f32[8,1024]{1,0:T(8,128)S(1)} %gather.15, f32[1024]{0:T(1024)S(1)} %iota_add_fusion, f32[8]{0:T(128)S(1)} %fusion.25, pred[8,8]{0,1:T(8,128)(4,1)S(1)} %copy.16), kind=kOutput, calls=%fused_computation.9 | convolution fusion | flops 103923712 | bytes 69728 | tf_op jit(solution)/shard_map/dot_general | solution.py:33
  (16 shorter events, 0.2 us)
Async XLA Ops:
  0.0 1.9 %copy-start = (bf16[6,256,1024]{2,1,0:T(8,128)(2,1)S(1)}, bf16[6,256,1024]{2,1,0:T(8,128)(2,1)}, u32[]{:S(2)}) copy-start(bf16[6,256,1024]{2,1,0:T(8,128)(2,1)} %param.5) | copy-start | bytes 9437188

commit v3 on v2

v3 whole, which is shorter than its diff:
```python
import functools
import math

import jax
import jax.numpy as jnp
from jax import lax
from jax.experimental import pallas as pl
from jax.experimental.pallas import tpu as pltpu
from jax.sharding import PartitionSpec as P

LANES = 128
PACK = 4608
MESH = pl.DeviceIdType.MESH


def kernel_table(rows, start, cols):
    row_pos = start + jnp.arange(rows, dtype=jnp.float32)[:, None]
    col_pos = jnp.arange(cols, dtype=jnp.float32)[None, :]
    return 1.0 / (row_pos - col_pos + 0.5)


def weigh(length, count, start):
    position = start + jnp.arange(count, dtype=jnp.float32)[None, :] + 0.5
    inside = position < length
    return (inside, jnp.sqrt(jnp.where(inside, position * (length - position), 1.0)))


def invert_block(sums, length, table, start):
    length = length.astype(jnp.float32)[:, None]
    col_in, col_w = weigh(length, sums.shape[1], 0.0)
    row_in, row_w = weigh(length, table.shape[0], start)
    scaled = jnp.where(col_in, col_w * sums, 0.0)
    image = jnp.dot(
        scaled, table.T, precision=lax.Precision.HIGHEST, preferred_element_type=jnp.float32
    )
    return jnp.where(row_in, image / (math.pi * row_w), 0.0)


def pick(table, index):
    hit = index[:, :, None] == jnp.arange(table.shape[1], dtype=jnp.int32)
    return jnp.sum(jnp.where(hit, table[:, None, :], 0), axis=-1)


def run_rings(rings):
    copies_at = []
    for s in range(max(r["n"] // 2 for r in rings)):
        copies = []
        for r in rings:
            n = r["n"]
            nr = n // 2
            nl = n - 1 - nr
            for go, steps, to, recv, send, sem in (
                (1, nr, r["right"], r["rr"], r["sr"], r["base"] + s),
                (-1, nl, r["left"], r["rl"], r["sl"], r["base"] + nr + s),
            ):
                if s >= steps:
                    continue
                dest = lax.rem(r["me"] + go * (steps - s) + 2 * n, n)
                if s == 0:
                    src = r["chunk"].at[dest]
                else:
                    send[s] = recv[s - 1] + r["chunk"][dest]
                    src = send.at[s]
                copy = pltpu.make_async_remote_copy(
                    src_ref=src,
                    dst_ref=recv.at[s],
                    send_sem=r["ssem"].at[sem],
                    recv_sem=r["rsem"].at[sem],
                    device_id=to,
                    device_id_type=MESH,
                )
                copy.start()
                copies.append(copy)
        for copy in copies:
            copy.wait()
    return [(r["rr"].at[r["n"] // 2 - 1], r["rl"].at[r["n"] - 2 - r["n"] // 2]) for r in rings]


def rs_kernel(ny, nz, xa, xb, oa, ob, s1a, s1b, *bufs):
    ssem, rsem = bufs[-2:]
    bufs = bufs[:-2]
    view = lax.axis_index("view")
    group = lax.axis_index("chord")
    y = view // nz
    z = lax.rem(view, nz)

    def dev(yy, zz):
        return (yy * nz + zz, group)

    z_right = dev(y, lax.rem(z + 1, nz))
    z_left = dev(y, lax.rem(z + nz - 1, nz))
    y_right = dev(lax.rem(y + 1, ny), z)
    y_left = dev(lax.rem(y + ny - 1, ny), z)

    barrier = pltpu.get_barrier_semaphore()
    for peer in (z_right, z_left, y_right, y_left):
        pl.semaphore_signal(barrier, inc=1, device_id=peer, device_id_type=MESH)
    pl.semaphore_wait(barrier, 4)

    def ring(n, me, right, left, chunk, at, base):
        rr, rl, sr, sl = bufs[4 * at: 4 * at + 4]
        return dict(n=n, me=me, right=right, left=left, chunk=chunk, rr=rr, rl=rl, sr=sr, sl=sl,
                    ssem=ssem, rsem=rsem, base=base)

    (ar, al), (br, bl) = run_rings([
        ring(nz, z, z_right, z_left, xa, 0, 0),
        ring(ny, y, y_right, y_left, xb, 1, nz - 1),
    ])
    s1a[...] = xa[z] + ar[...] + al[...]
    s1b[...] = xb[y] + br[...] + bl[...]
    (ar, al), (br, bl) = run_rings([
        ring(ny, y, y_right, y_left, s1a, 2, nz + ny - 2),
        ring(nz, z, z_right, z_left, s1b, 3, nz + 2 * ny - 3),
    ])
    oa[...] = s1a[y] + ar[...] + al[...]
    ob[...] = s1b[z] + br[...] + bl[...]


def reduce_scatter(xa, xb, ny, nz):
    ra, rb = xa.shape[2], xb.shape[2]
    f32 = jnp.float32

    def slots(n, shape):
        return [pltpu.VMEM((n // 2,) + shape, f32), pltpu.VMEM((n - 1 - n // 2,) + shape, f32)] * 2

    bufs = (
        slots(nz, (ny, ra, LANES)) + slots(ny, (nz, rb, LANES))
        + slots(ny, (ra, LANES)) + slots(nz, (rb, LANES))
    )
    return pl.pallas_call(
        functools.partial(rs_kernel, ny, nz),
        out_shape=(jax.ShapeDtypeStruct((ra, LANES), f32), jax.ShapeDtypeStruct((rb, LANES), f32)),
        in_specs=[pl.BlockSpec(memory_space=pltpu.VMEM)] * 2,
        out_specs=(pl.BlockSpec(memory_space=pltpu.VMEM),) * 2,
        scratch_shapes=[pltpu.VMEM((ny, ra, LANES), f32), pltpu.VMEM((nz, rb, LANES), f32)]
        + bufs
        + [pltpu.SemaphoreType.DMA((2 * (nz + ny - 2),)), pltpu.SemaphoreType.DMA((2 * (nz + ny - 2),))],
        compiler_params=pltpu.CompilerParams(collective_id=0, has_side_effects=True),
    )(xa, xb)


def per_device(ny, nz, proj, tiles, owner, lengths):
    view_count, group_rows, footprint = proj.shape
    samples = tiles.shape[2]
    group = lax.axis_index("chord")
    view_place = lax.axis_index("view")
    view_devices = ny * nz
    owned = group_rows // view_devices
    chunks_per_row = samples // LANES
    slots = min(chunks_per_row * owned, (PACK + owned * (LANES - 1)) // LANES)

    tile_rows = tiles.reshape(view_count, footprint, chunks_per_row, LANES)
    sums = jnp.einsum("vkd,vdcl->kcl", proj, tile_rows, preferred_element_type=jnp.float32)

    my_order = lax.dynamic_index_in_dim(owner, group, 0, keepdims=False)
    my_lengths = lax.dynamic_index_in_dim(lengths, group, 0, keepdims=False)
    order_len = pick(my_lengths[None, :], my_order[None, :])
    order_len = order_len.reshape(view_devices, owned)
    order_rows = my_order.reshape(view_devices, owned)

    counts = (order_len + LANES - 1) // LANES
    ends = jnp.cumsum(counts, axis=1)
    starts = ends - counts
    slot = jnp.arange(slots, dtype=jnp.int32)
    member = jnp.sum((ends[:, None, :] <= slot[None, :, None]).astype(jnp.int32), axis=2)
    member = jnp.minimum(member, owned - 1)
    first = pick(starts, member)
    src_row = pick(order_rows, member)
    within = jnp.clip(slot[None, :] - first, 0, chunks_per_row - 1)
    src = src_row * chunks_per_row + within
    src = src.reshape(ny, nz, slots)
    half = (slots + 1) // 2
    flat = sums.reshape(group_rows * chunks_per_row, LANES)
    xa = jnp.take(flat, src[:, :, :half].transpose(1, 0, 2), axis=0)
    xb = jnp.take(flat, src[:, :, half:], axis=0)

    mine = jnp.concatenate(reduce_scatter(xa, xb, ny, nz), axis=0)

    my_starts = lax.dynamic_index_in_dim(starts, view_place, 0, keepdims=False)
    my_len = lax.dynamic_index_in_dim(order_len, view_place, 0, keepdims=False)
    back = my_starts[:, None] + jnp.arange(chunks_per_row, dtype=jnp.int32)[None, :]
    back = jnp.minimum(back, slots - 1)
    rows = jnp.take(mine, back.reshape(-1), axis=0).reshape(owned, samples)

    table = kernel_table(samples, 0.0, samples)
    recon = invert_block(rows, my_len, table, 0.0)
    return recon[None]


def solution(mesh):
    view_devices = mesh.shape["view"]
    ny = int(round(math.sqrt(view_devices)))
    nz = view_devices // ny
    placed = (P("view", "chord", None), P("view", None, None), P(), P())
    return jax.shard_map(
        functools.partial(per_device, ny, nz),
        mesh=mesh,
        in_specs=placed,
        out_specs=P("chord", "view", None),
        check_vma=False,
    )
```

time: 80.1 us -> 72.5 us (0.905)
  Pallas kernels: 48.4 us -> 44.1 us
  matrix products: 8.85 us -> 6.14 us
  local copies, waits for them, and re-layouts: 18.7 us -> 17.6 us
    pallas_call x1, Pallas kernels: 48.4 us -> 44.1 us  [reduce_scatter(): pl.pallas_call(functools.partial(rs_kernel, ny, nz), out_shape=(jax.Shape...]
    reshape x2 -> x0, local copies, waits for them, and re-layouts: 2.88 us -> none  [the longest x1 2.74 us: per_device(): flat = sums.reshape(group_rows * chunks_per_row, LANES)]
    dot_general x1, matrix products: 4.49 us -> 1.79 us  [per_device(): jnp.einsum('vkd,vdcl->kcl', proj, tile_rows, preferred_element_type=jnp.f...]
    dot_general x0 -> x1, local copies, waits for them, and re-layouts: none -> 2.57 us  [per_device(): jnp.einsum('vkd,vdcl->kcl', proj, tile_rows, preferred_element_type=jnp.f...]
    gather x2 -> x4, local copies, waits for them, and re-layouts: 10 us -> 8.64 us  [the longest x2 4.34 us: per_device(): xa = jnp.take(flat, src[:, :, :half].transpose(1, 0, 2), axis=0)]
    unnamed x2 -> x3, local copies, waits for them, and re-layouts: 1.89 us -> 2.83 us
    select_n x2 -> x4, other arithmetic: 2.64 us -> 2.41 us  [the longest x2 1.22 us: per_device(): xb = jnp.take(flat, src[:, :, half:], axis=0)]
where the time goes in v3:
time: 72.5 us; the launch traced here: 72.1 us
  Pallas kernels  44.1 us (61%)
  local copies, waits for them, and re-layouts  17.6 us (24%)
  matrix products  6.14 us (8%)
  other arithmetic  4.14 us (6%)
    pallas_call x1, Pallas kernels, reduce_scatter(): pl.pallas_call(functools.partial(rs_kernel, ny, nz), out_shape=(jax.Shape...  44.1 us
    dot_general x1, matrix products, invert_block(): jnp.dot(scaled, table.T, precision=lax.Precision.HIGHEST, preferred_eleme...  4.35 us
    gather x2, local copies, waits for them, and re-layouts, per_device(): xa = jnp.take(flat, src[:, :, :half].transpose(1, 0, 2), axis=0)  4.34 us
    gather x2, local copies, waits for them, and re-layouts, per_device(): xb = jnp.take(flat, src[:, :, half:], axis=0)  4.3 us
    unnamed x3, local copies, waits for them, and re-layouts  2.83 us
    dot_general x1, local copies, waits for them, and re-layouts, per_device(): jnp.einsum('vkd,vdcl->kcl', proj, tile_rows, preferred_element_type=jnp.f...  2.57 us
    dynamic_slice x2, local copies, waits for them, and re-layouts, per_device(): my_order = lax.dynamic_index_in_dim(owner, group, 0, keepdims=False)  1.91 us
    dot_general x1, matrix products, per_device(): jnp.einsum('vkd,vdcl->kcl', proj, tile_rows, preferred_element_type=jnp.f...  1.79 us

profile of v3, /device:TPU:6, one launch (start us, length us, event | category | flops | bytes accessed | tf_op | source)
XLA Modules:
  0.0 72.1 jit_solution(1594958185227551870)
XLA Ops:
  0.0 0.0 copy-start
  0.0 2.8 %copy.28 = bf16[192,8,8,128]{3,2,1,0:T(8,128)(2,1)S(1)} copy(bf16[192,8,8,128]{3,1,2,0:T(8,128)(2,1)} %bitcast.44) | data formatting | bytes 6291456
  2.8 0.0 copy-done
  2.8 1.8 %fusion.5 = f32[512,8,128]{2,0,1:T(8,128)S(1)} fusion(bf16[12,128,8,128]{3,2,1,0:T(8,128)(2,1)S(1)} %bitcast.45, bf16[12,512,128]{2,1,0:T(8,128)(2,1)S(1)} %copy-done), kind=kOutput, calls=%fused_computation.10 | convolution fusion | flops 1610612736 | bytes 6815744 | tf_op jit(solution)/shard_map/vkd,vdcl->kcl/dot_general | solution.py:153
  4.6 2.6 %copy.34 = f32[512,8,128]{2,1,0:T(8,128)} copy(f32[512,8,128]{2,0,1:T(8,128)S(1)} %fusion.5) | data formatting | bytes 4194304 | tf_op jit(solution)/shard_map/vkd,vdcl->kcl/dot_general | solution.py:153
  7.2 0.5 broadcast.194
  7.7 1.4 %fusion.38 = (s32[512]{0:T(512)S(1)}, s32[1,512]{1,0:T(1,128)S(1)}, s32[1,512]{1,0:T(1,128)S(1)}) fusion(s32[]{:T(128)} %broadcast.194, s32[8,512]{1,0:T(8,128)} %param.6, s32[]{:T(128)S(6)} %select_n.89, s32[8,512]{1,0:T(8,128)} %param.7), kind=kLoop, calls=%fused_computation.77 | loop fusion | bytes 10248 | tf_op jit(solution)/shard_map/jit(dynamic_index_in_dim)/dynamic_slice | solution.py:155
  9.1 0.1 broadcast_in_dim.104
  9.2 0.1 copy.19
  9.3 0.3 select_reduce_fusion
  9.5 0.1 reshape.191
  9.7 0.2 reduce_window_sum.11
  9.8 0.1 copy.18
  9.9 0.1 convert_reduce_fusion
  10.0 0.1 copy.21
  10.1 0.1 select_reduce_fusion.2
  10.2 0.1 copy.22
  10.3 0.1 copy.20
  10.4 0.1 reshape.196
  10.6 4.3 %gather_fusion = f32[1408,128]{1,0:T(8,128)S(1)} fusion(f32[4096,128]{1,0:T(8,128)} %bitcast.42, s32[2048]{0:T(1024)S(1)} %pad_clamp_fusion.1), kind=kCustom, calls=%fused_computation | custom fusion | bytes 1447424 | tf_op jit(solution)/shard_map/jit(_take)/gather | solution.py:174
  14.9 0.1 reshape.195
  15.0 1.2 %broadcast_select_fusion.1.xa = f32[8,8,22,128]{3,2,1,0:T(8,128)} fusion(f32[8,8,22,128]{3,2,1,0:T(8,128)S(1)} %reshape.195, pred[8,8,22]{2,1,0:T(8,128)(4,1)S(1)} %copy.23), kind=kLoop, calls=%fused_computation.18 | loop fusion | flops 180224 | bytes 1443200 | tf_op jit(solution)/shard_map/jit(_take)/select_n | solution.py:174
  16.2 0.1 compare_select_fusion
  16.2 0.1 reshape.204
  16.4 4.2 %gather_fusion.1 = f32[1344,128]{1,0:T(8,128)S(1)} fusion(f32[4096,128]{1,0:T(8,128)} %bitcast.43, s32[2048]{0:T(1024)S(1)} %pad_clamp_fusion), kind=kCustom, calls=%fused_computation.1 | custom fusion | bytes 1381632 | tf_op jit(solution)/shard_map/jit(_take)/gather | solution.py:175
  20.6 0.1 reshape.203
  20.7 0.1 compare_and_fusion
  20.8 1.1 %broadcast_select_fusion.xb = f32[8,8,21,128]{3,2,1,0:T(8,128)} fusion(f32[8,8,21,128]{3,2,1,0:T(8,128)S(1)} %reshape.203, pred[8,8,21]{2,1,0:T(8,128)(4,1)S(1)} %compare_and_fusion), kind=kLoop, calls=%fused_computation.17 | loop fusion | flops 172032 | bytes 1377600 | tf_op jit(solution)/shard_map/jit(_take)/select_n | solution.py:175
  22.0 44.1 %shard_map.46 = (f32[22,128]{1,0:T(8,128)}, f32[21,128]{1,0:T(8,128)}) custom-call(f32[8,8,22,128]{3,2,1,0:T(8,128)} %broadcast_select_fusion.1.xa, f32[8,8,21,128]{3,2,1,0:T(8,128)} %broadcast_select_fusion.xb), custom_call_target="tpu_custom_call" | custom-call | tf_op jit(solution)/shard_map/pallas_call | solution.py:130
  66.0 0.7 %pad_maximum_fusion = f32[43,128]{1,0:T(8,128)S(1)} fusion(f32[21,128]{1,0:T(8,128)} %get-tuple-element.8, f32[22,128]{1,0:T(8,128)} %get-tuple-element.7), kind=kLoop, calls=%fused_computation.47 | loop fusion | flops 5504 | bytes 44032 | tf_op jit(solution)/shard_map/concatenate | solution.py:177
  66.8 0.1 add_minimum_fusion
  66.8 0.1 min.44
  66.9 0.6 gather_fusion.2
  67.6 0.1 compare_and_fusion.2
  67.7 0.1 copy.17
  67.8 4.4 %fusion.11 = f32[1,8,1024]{2,1,0:T(8,128)} fusion(f32[8,1024]{1,0:T(8,128)S(1)} %gather.17, f32[1024]{0:T(1024)S(1)} %iota_add_fusion, f32[8]{0:T(128)S(1)} %fusion.30, pred[8,8]{0,1:T(8,128)(4,1)S(1)} %copy.17), kind=kOutput, calls=%fused_computation.14 | convolution fusion | flops 103923712 | bytes 69728 | tf_op jit(solution)/shard_map/dot_general | solution.py:33
  (17 shorter events, 0.2 us)
Async XLA Ops:
  0.0 2.8 %copy-start = (bf16[12,512,128]{2,1,0:T(8,128)(2,1)S(1)}, bf16[12,512,128]{2,1,0:T(8,128)(2,1)}, u32[]{:S(2)}) copy-start(bf16[12,512,128]{2,1,0:T(8,128)(2,1)} %param.4) | copy-start | bytes 4718596
